TPU v7x, 32 devices: a whole 2x2x4 slice. The times are simulated.
32 devices in a mesh: heads: 4 (over y, x), seq: 8 (over z, core).
Axes of the slice: x: 2, y: 2, z: 4, core: 2. Of those that a mesh axis runs over, the one named last changes fastest.
Arguments:
- tokens: bfloat16 [7168, 2048], P('seq'), may hold values from -6 to 6
- w_qkv: bfloat16 [2048, 3, 2048], P(None, None, 'heads'), may hold values from -0.1875 to 0.1875
- w_out: bfloat16 [2048, 2048], P('heads'), may hold values from -0.75 to 0.75
- w_up: bfloat16 [2048, 8192], P('seq', 'heads'), may hold values from -0.125 to 0.125
- w_down: bfloat16 [8192, 2048], P('heads', 'seq'), may hold values from -0.0625 to 0.0625
- gain_attn: float32 [2048], replicated, may hold values from 0.1 to 1.9
- gain_ffn: float32 [2048], replicated, may hold values from 0.1 to 1.9
- w_router: float32 [2048, 8], replicated, may hold values from -0.25 to 0.25
- head_quarters: int32 [5], replicated, may hold values from 1 to 4, as said below
- ffn_quarters: int32 [5], replicated, may hold values from 1 to 4, as said below
- router_targets: int32 [5, 2], replicated, may hold values from 0 to 3
- cotangent: bfloat16 [7168, 2048], P('seq'), may hold values from -6 to 6
Outputs:
- output: bfloat16 [7168, 2048], P('seq')
- grad_tokens: float32 [7168, 2048], P('seq')
- grad_qkv: float32 [2048, 3, 2048], P(None, None, 'heads')
- grad_out: float32 [2048, 2048], P('heads')
- grad_up: float32 [2048, 8192], P('seq', 'heads')
- grad_down: float32 [8192, 2048], P('heads', 'seq')
- grad_gain_attn: float32 [2048], replicated
- grad_gain_ffn: float32 [2048], replicated
- grad_router: float32 [2048, 8], replicated
Inputs may be any that keep to these rules, and one draw needn't show every extreme that they name: Sequence s uses the first head_quarters[s] * 4 heads; some sequence uses all heads and some a quarter of them. Sequence s uses the first ffn_quarters[s] * 2048 hidden units; some sequence uses all and some a quarter.
All inputs are finite; a program needn't handle non-finite values.
Results may differ from a plain program's by a relative error of at most 0.023.
Values may be sent and summed in bfloat16 or wider, within the bound.
No kernel may reach another device: no remote copies, remote signals or barrier semaphores. Data moves between devices by JAX's collectives and lax.ppermute only.
A program may use at most 256 MiB of HBM per device.

v0:
```python
import jax
import jax.numpy as jnp
from jax import lax
from jax.sharding import PartitionSpec as P

D = 2048
H = 16
HD = 128
FF = 8192
SHORT_DEV = 128
NSHORT = 3
NLONG = 2
LEVELS = 4
SEQS = 5
epsilon = 1e-05
highest = lax.Precision.HIGHEST


def normalize_parts(values):
    centered = values - jnp.mean(values, axis=-1, keepdims=True)
    inverse = lax.rsqrt(jnp.mean(centered * centered, axis=-1, keepdims=True) + epsilon)
    return (centered * inverse, inverse)


def normalize_back(grad_normed, normed_hat, inverse, gain):
    grad_hat = grad_normed * gain
    middle = (
        grad_hat
        - jnp.mean(grad_hat, axis=-1, keepdims=True)
        - normed_hat * jnp.mean(grad_hat * normed_hat, axis=-1, keepdims=True)
    )
    return (inverse * middle, jnp.sum(grad_normed * normed_hat, axis=0))


def rotate(values, cosine, sine, inverse_turn):
    row_count = values.shape[0]
    shaped = values.reshape(row_count, -1, HD)
    half_dim = HD // 2
    former = shaped[..., :half_dim]
    latter = shaped[..., half_dim:]
    if inverse_turn:
        turned = [former * cosine + latter * sine, latter * cosine - former * sine]
    else:
        turned = [former * cosine - latter * sine, latter * cosine + former * sine]
    return jnp.concatenate(turned, axis=-1).reshape(row_count, -1)


def gather_rows(keys, values):
    return (
        lax.all_gather(keys, "seq", axis=1, tiled=True),
        lax.all_gather(values, "seq", axis=1, tiled=True),
    )


def masked_scores(query, keys, first_pos):
    seq_number, seq_size = (query.shape[0], query.shape[1])
    length = keys.shape[1]
    query_heads = query.reshape(seq_number, seq_size, -1, HD)
    key_heads = keys.reshape(seq_number, length, -1, HD)
    scores = jnp.einsum(
        "cqhd,ckhd->chqk", query_heads, key_heads, preferred_element_type=jnp.float32
    ) * HD ** (-0.5)
    allowed = jnp.arange(length)[None, :] <= (first_pos + jnp.arange(seq_size))[:, None]
    return (jnp.where(allowed[None, None], scores, -1e30), query_heads, key_heads)


def attend_forward(query, keys, values, first_pos):
    seq_number, seq_size = (query.shape[0], query.shape[1])
    scores, query_heads, key_heads = masked_scores(query, keys, first_pos)
    largest = jnp.max(scores, axis=-1, keepdims=True)
    raised = jnp.exp(scores - largest)
    total = jnp.sum(raised, axis=-1, keepdims=True)
    probs = (raised / total).astype(jnp.bfloat16)
    value_heads = values.reshape(seq_number, values.shape[1], -1, HD)
    mixed = jnp.einsum("chqk,ckhd->cqhd", probs, value_heads, preferred_element_type=jnp.float32)
    return (mixed.reshape(seq_number, seq_size, -1), largest + jnp.log(total))


def attend_backward(query, keys, values, grad_mixed, log_total, first_pos):
    seq_number, seq_size = (query.shape[0], query.shape[1])
    length = keys.shape[1]
    scores, query_heads, key_heads = masked_scores(query, keys, first_pos)
    probs = jnp.exp(scores - log_total)
    value_heads = values.reshape(seq_number, length, -1, HD)
    grad_heads = grad_mixed.reshape(seq_number, seq_size, -1, HD)
    grad_probs = jnp.einsum(
        "cqhd,ckhd->chqk", grad_heads, value_heads, preferred_element_type=jnp.float32
    )
    delta = jnp.sum(probs * grad_probs, axis=-1)
    grad_scores = (probs * (grad_probs - delta[..., None])).astype(jnp.bfloat16)
    grad_query = jnp.einsum(
        "chqk,ckhd->cqhd", grad_scores, key_heads, preferred_element_type=jnp.float32
    ) * HD ** (-0.5)
    grad_query = grad_query.reshape(seq_number, seq_size, -1)
    return (grad_query, delta)


def attend_key_side(query_all, keys, values, grad_all, total_all, delta_all, key_first):
    seq_number, length = (query_all.shape[0], query_all.shape[1])
    key_count = keys.shape[1]
    query_heads = query_all.reshape(seq_number, length, -1, HD)
    key_heads = keys.reshape(seq_number, key_count, -1, HD)
    value_heads = values.reshape(seq_number, key_count, -1, HD)
    grad_heads = grad_all.reshape(seq_number, length, -1, HD)
    scores = jnp.einsum(
        "cqhd,ckhd->chqk", query_heads, key_heads, preferred_element_type=jnp.float32
    ) * HD ** (-0.5)
    allowed = (key_first + jnp.arange(key_count))[None, :] <= jnp.arange(length)[:, None]
    scores = jnp.where(allowed[None, None], scores, -1e30)
    probs = jnp.exp(scores - total_all[..., None])
    probs_low = probs.astype(jnp.bfloat16)
    grad_probs = jnp.einsum(
        "cqhd,ckhd->chqk", grad_heads, value_heads, preferred_element_type=jnp.float32
    )
    grad_scores = (probs * (grad_probs - delta_all[..., None])).astype(jnp.bfloat16)
    grad_values = jnp.einsum(
        "chqk,cqhd->ckhd", probs_low, grad_heads, preferred_element_type=jnp.float32
    )
    grad_keys = jnp.einsum(
        "chqk,cqhd->ckhd", grad_scores, query_heads, preferred_element_type=jnp.float32
    ) * HD ** (-0.5)
    return (
        grad_keys.reshape(seq_number, key_count, -1),
        grad_values.reshape(seq_number, key_count, -1),
    )


def local(
    tokens,
    w_qkv,
    w_out,
    w_up,
    w_down,
    gain_attn,
    gain_ffn,
    w_router,
    head_quarters,
    ffn_quarters,
    router_targets,
    cotangent,
):
    row_count = tokens.shape[0]
    seq_rank = lax.axis_index("seq")
    seq_count = lax.axis_size("seq")
    head_rank = lax.axis_index("heads")
    head_width = w_out.shape[0]
    ffn_width = w_up.shape[1]
    short_rows = NSHORT * SHORT_DEV
    column = jnp.arange(row_count)
    is_short = column < short_rows
    offset = column - short_rows
    seq_id = jnp.where(is_short, column // SHORT_DEV, NSHORT + offset // (2 * SHORT_DEV))
    position = jnp.where(
        is_short,
        seq_rank * SHORT_DEV + column % SHORT_DEV,
        seq_rank * 2 * SHORT_DEV + offset % (2 * SHORT_DEV),
    )
    in_seq = seq_id[:, None] == jnp.arange(SEQS)[None, :]
    member = in_seq.astype(jnp.float32)
    seq_length = jnp.where(
        jnp.arange(SEQS) < NSHORT, SHORT_DEV * seq_count, 2 * SHORT_DEV * seq_count
    ).astype(jnp.float32)
    head_level = jnp.sum(jnp.where(in_seq, head_quarters[None, :], 0), axis=1)
    ffn_level = jnp.sum(jnp.where(in_seq, ffn_quarters[None, :], 0), axis=1)
    head_index = head_rank * (head_width // HD) + jnp.arange(head_width) // HD
    head_live = (head_index[None, :] < (head_level * (H // LEVELS))[:, None]).astype(jnp.bfloat16)
    unit_index = head_rank * ffn_width + jnp.arange(ffn_width)
    ffn_live = (unit_index[None, :] < (ffn_level * (FF // LEVELS))[:, None]).astype(jnp.float32)
    half_dim = HD // 2
    frequency = 10000.0 ** (-jnp.arange(half_dim, dtype=jnp.float32) * 2.0 / HD)
    angle = position.astype(jnp.float32)[:, None] * frequency[None, :]
    cosine = jnp.cos(angle)[:, None, :]
    sine = jnp.sin(angle)[:, None, :]
    tokens_wide = tokens.astype(jnp.float32)
    hat_one, inverse_one = normalize_parts(tokens_wide)
    normed_one = hat_one * gain_attn
    normed_low = normed_one.astype(jnp.bfloat16)
    flat_qkv = w_qkv.reshape(D, -1)
    projected = jnp.dot(normed_low, flat_qkv, preferred_element_type=jnp.float32).reshape(
        row_count, 3, head_width
    )
    query = rotate(projected[:, 0], cosine, sine, False).astype(jnp.bfloat16)
    keys = rotate(projected[:, 1], cosine, sine, False).astype(jnp.bfloat16)
    values = projected[:, 2].astype(jnp.bfloat16)
    partial_pool = jnp.dot(
        member.T, normed_one, precision=highest, preferred_element_type=jnp.float32
    )
    pooled = (
        lax.psum(partial_pool.astype(jnp.bfloat16), "seq").astype(jnp.float32)
        * lax.rsqrt(seq_length)[:, None]
    )
    shape_list = ((0, NSHORT, SHORT_DEV), (short_rows, NLONG, 2 * SHORT_DEV))
    saved_parts = []
    mixed_parts = []
    for row_start, seq_number, seq_size in shape_list:
        row_stop = row_start + seq_number * seq_size
        piece_query = query[row_start:row_stop].reshape(seq_number, seq_size, head_width)
        piece_keys = keys[row_start:row_stop].reshape(seq_number, seq_size, head_width)
        piece_values = values[row_start:row_stop].reshape(seq_number, seq_size, head_width)
        gathered_keys, gathered_values = gather_rows(piece_keys, piece_values)
        mixed, log_total = attend_forward(
            piece_query, gathered_keys, gathered_values, seq_rank * seq_size
        )
        saved_parts.append(
            (piece_query, piece_keys, piece_values, gathered_keys, gathered_values, log_total)
        )
        mixed_parts.append(mixed.reshape(seq_number * seq_size, head_width))
    heads_out = (jnp.concatenate(mixed_parts, axis=0) * head_live).astype(jnp.bfloat16)
    attn_part = jnp.dot(heads_out, w_out, preferred_element_type=jnp.float32)
    hidden = tokens_wide + lax.psum(attn_part, "heads")
    hat_two, inverse_two = normalize_parts(hidden)
    normed_two = (hat_two * gain_ffn).astype(jnp.bfloat16)
    full_up, full_down = (
        lax.all_gather(w_up, "seq", axis=0, tiled=True),
        lax.all_gather(w_down, "seq", axis=1, tiled=True),
    )
    upward = jnp.dot(normed_two, full_up, preferred_element_type=jnp.float32)
    active = (jnp.square(jnp.maximum(upward, 0.0)) * ffn_live).astype(jnp.bfloat16)
    ffn_part = jnp.dot(active, full_down, preferred_element_type=jnp.float32)
    output = (hidden + lax.psum(ffn_part.astype(jnp.bfloat16), "heads").astype(jnp.float32)).astype(
        jnp.bfloat16
    )
    back_up, back_down = (
        lax.all_gather(w_up, "seq", axis=0, tiled=True),
        lax.all_gather(w_down, "seq", axis=1, tiled=True),
    )
    upward_again = jnp.dot(normed_two, back_up, preferred_element_type=jnp.float32)
    active_again = (jnp.square(jnp.maximum(upward_again, 0.0)) * ffn_live).astype(jnp.bfloat16)
    grad_active = jnp.dot(cotangent, back_down.T, preferred_element_type=jnp.float32).astype(
        jnp.bfloat16
    )
    grad_upward = (
        grad_active.astype(jnp.float32) * ffn_live * 2.0 * jnp.maximum(upward_again, 0.0)
    ).astype(jnp.bfloat16)
    grad_down_part = jnp.dot(active_again.T, cotangent, preferred_element_type=jnp.float32)
    grad_up_part = jnp.dot(normed_two.T, grad_upward, preferred_element_type=jnp.float32)
    grad_two = lax.psum(
        jnp.dot(grad_upward, back_up.T, preferred_element_type=jnp.float32), "heads"
    )
    grad_up, grad_down = (
        lax.psum_scatter(
            grad_up_part.astype(jnp.bfloat16), "seq", scatter_dimension=0, tiled=True
        ).astype(jnp.float32),
        lax.psum_scatter(
            grad_down_part.astype(jnp.bfloat16), "seq", scatter_dimension=1, tiled=True
        ).astype(jnp.float32),
    )
    back_two, grad_gain_two = normalize_back(grad_two, hat_two, inverse_two, gain_ffn)
    grad_hidden = cotangent.astype(jnp.float32) + back_two
    grad_attn = grad_hidden.astype(jnp.bfloat16)
    grad_out_part = jnp.dot(heads_out.T, grad_attn, preferred_element_type=jnp.float32)
    grad_heads = (
        jnp.dot(grad_attn, w_out.T, preferred_element_type=jnp.float32).astype(jnp.bfloat16)
        * head_live
    )
    query_grads = []
    key_grads = []
    value_grads = []
    for shape_entry, saved in zip(shape_list, saved_parts):
        row_start, seq_number, seq_size = shape_entry
        piece_query, piece_keys, piece_values, gathered_keys, gathered_values, log_total = saved
        piece_grad = grad_heads[row_start : row_start + seq_number * seq_size].reshape(
            seq_number, seq_size, head_width
        )
        grad_query, delta = attend_backward(
            piece_query, gathered_keys, gathered_values, piece_grad, log_total, seq_rank * seq_size
        )
        query_all, grad_all = (
            lax.all_gather(piece_query, "seq", axis=1, tiled=True),
            lax.all_gather(piece_grad, "seq", axis=1, tiled=True),
        )
        total_all, delta_all = (
            lax.all_gather(log_total[..., 0], "seq", axis=2, tiled=True),
            lax.all_gather(delta, "seq", axis=2, tiled=True),
        )
        local_keys, local_values = attend_key_side(
            query_all, piece_keys, piece_values, grad_all, total_all, delta_all, seq_rank * seq_size
        )
        query_grads.append(grad_query.reshape(seq_number * seq_size, head_width))
        key_grads.append(local_keys.reshape(seq_number * seq_size, head_width))
        value_grads.append(local_values.reshape(seq_number * seq_size, head_width))
    grad_query_all = rotate(jnp.concatenate(query_grads, axis=0), cosine, sine, True)
    grad_key_all = rotate(jnp.concatenate(key_grads, axis=0), cosine, sine, True)
    grad_value_all = jnp.concatenate(value_grads, axis=0)
    grad_projected = (
        jnp.stack([grad_query_all, grad_key_all, grad_value_all], axis=1)
        .astype(jnp.bfloat16)
        .reshape(row_count, -1)
    )
    grad_qkv_part = jnp.dot(
        normed_low.T, grad_projected, preferred_element_type=jnp.float32
    ).reshape(D, 3, head_width)
    grad_one = lax.psum(
        jnp.dot(grad_projected, flat_qkv.T, preferred_element_type=jnp.float32).astype(
            jnp.bfloat16
        ),
        "heads",
    ).astype(jnp.float32)
    logits = jnp.dot(pooled, w_router, precision=highest, preferred_element_type=jnp.float32)
    logit_grads = []
    for group in range(2):
        group_logits = logits[:, LEVELS * group : LEVELS * (group + 1)]
        raised = jnp.exp(group_logits - jnp.max(group_logits, axis=1, keepdims=True))
        chosen = (jnp.arange(LEVELS)[None, :] == router_targets[:, group][:, None]).astype(
            jnp.float32
        )
        logit_grads.append(raised / jnp.sum(raised, axis=1, keepdims=True) - chosen)
    grad_logits = jnp.concatenate(logit_grads, axis=1)
    grad_router = jnp.dot(
        pooled.T, grad_logits, precision=highest, preferred_element_type=jnp.float32
    )
    grad_pooled = (
        jnp.dot(grad_logits, w_router.T, precision=highest, preferred_element_type=jnp.float32)
        * lax.rsqrt(seq_length)[:, None]
    )
    grad_one = grad_one + jnp.dot(
        member, grad_pooled, precision=highest, preferred_element_type=jnp.float32
    )
    back_one, grad_gain_one = normalize_back(grad_one, hat_one, inverse_one, gain_attn)
    grad_tokens = grad_hidden + back_one
    grad_qkv, grad_out, grad_gain_attn, grad_gain_ffn = (
        lax.psum(grad_qkv_part.astype(jnp.bfloat16), "seq").astype(jnp.float32),
        lax.psum(grad_out_part.astype(jnp.bfloat16), "seq").astype(jnp.float32),
        lax.psum(grad_gain_one.astype(jnp.bfloat16), "seq").astype(jnp.float32),
        lax.psum(grad_gain_two.astype(jnp.bfloat16), "seq").astype(jnp.float32),
    )
    return (
        output,
        grad_tokens,
        grad_qkv,
        grad_out,
        grad_up,
        grad_down,
        grad_gain_attn,
        grad_gain_ffn,
        grad_router,
    )


def solution(mesh):
    return jax.shard_map(
        local,
        mesh=mesh,
        in_specs=(
            P("seq", None),
            P(None, None, "heads"),
            P("heads", None),
            P("seq", "heads"),
            P("heads", "seq"),
            P(),
            P(),
            P(),
            P(),
            P(),
            P(),
            P("seq", None),
        ),
        out_specs=(
            P("seq", None),
            P("seq", None),
            P(None, None, "heads"),
            P("heads", None),
            P("seq", "heads"),
            P("heads", "seq"),
            P(),
            P(),
            P(),
        ),
        check_vma=False,
    )
```

profile of v0, /device:TPU:0, one launch (start us, length us, event | category | flops | bytes accessed | tf_op | source)
XLA Modules:
  0.0 1484.3 jit_solution(1231842556310068782)
XLA Ops:
  81.1 34.7 %all-gather.13.cloned.1.call-done = bf16[3,1024,512]{2,1,0:T(8,128)(2,1)} async-done(((bf16[3,128,512]{2,1,0:T(8,128)(2,1)}), bf16[3,1024,512]{2,1,0:T(8,128)(2,1)}) %all-gather.13.cloned.1.call-update) | async-done | bytes 3145744 | tf_op jit(solution)/shard_map/all_gather | solution.py:50
  134.2 29.5 %all-gather.17.cloned.1.call-done = bf16[2,2048,512]{2,1,0:T(8,128)(2,1)} async-done(((bf16[2,256,512]{2,1,0:T(8,128)(2,1)}), bf16[2,2048,512]{2,1,0:T(8,128)(2,1)}) %all-gather.17.cloned.1.call-update) | async-done | bytes 4194320 | tf_op jit(solution)/shard_map/all_gather | solution.py:50
  185.6 25.3 %all-gather.15.cloned.1.call-done = bf16[2,2048,512]{2,1,0:T(8,128)(2,1)} async-done(((bf16[2,256,512]{2,1,0:T(8,128)(2,1)}), bf16[2,2048,512]{2,1,0:T(8,128)(2,1)}) %all-gather.15.cloned.1.call-update) | async-done | bytes 4194320 | tf_op jit(solution)/shard_map/all_gather | solution.py:51
  240.7 153.0 %all-reduce.8.cloned.1.call-done = f32[896,2048]{1,0:T(8,128)} async-done(((f32[896,2048]{1,0:T(8,128)}), f32[896,2048]{1,0:T(8,128)}) %all-reduce.8.cloned.1.call-update) | async-done | bytes 7340048 | tf_op jit(solution)/shard_map/psum | solution.py:210
  402.5 74.7 %all-gather.19.cloned.1.call-done = bf16[2048,2048]{1,0:T(8,128)(2,1)} async-done(((bf16[256,2048]{1,0:T(8,128)(2,1)}), bf16[2048,2048]{1,0:T(8,128)(2,1)}) %all-gather.19.cloned.1.call-update) | async-done | bytes 8388624 | tf_op jit(solution)/shard_map/all_gather | solution.py:214
  477.2 14.6 fusion.154
  491.8 67.9 %all-gather.21.cloned.1.call-done = bf16[2048,2048]{1,0:T(8,128)(2,1)} async-done(((bf16[2048,256]{1,0:T(8,128)(2,1)}), bf16[2048,2048]{1,0:T(8,128)(2,1)}) %all-gather.21.cloned.1.call-update) | async-done | bytes 8388624 | tf_op jit(solution)/shard_map/all_gather | solution.py:215
  559.8 15.0 %fusion.29 = bf16[896,2048]{1,0:T(8,128)(2,1)} fusion(f32[896,2048]{1,0:T(8,128)} %fusion.154, s32[2048]{0:T(1024)S(1)} %iota_add_fusion, s32[896]{0:T(1024)S(1)} %broadcast_multiply_fusion, bf16[896,2048]{1,0:T(8,128)(2,1)} %param.23, bf16[2048,2048]{1,0:T(8,128)(2,1)} %all-gather.21.cloned.1.call-done), kind=kOutput, calls=%fused_computation.42 | convolution fusion | flops 7530872832 | bytes 23080448 | tf_op jit(solution)/shard_map/dot_general | solution.py:229
  593.4 146.5 %all-reduce.10.cloned.1.call-done = f32[896,2048]{1,0:T(8,128)} async-done(((f32[896,2048]{1,0:T(8,128)}), f32[896,2048]{1,0:T(8,128)}) %all-reduce.10.cloned.1.call-update) | async-done | bytes 7340048 | tf_op jit(solution)/shard_map/psum | solution.py:237
  760.6 15.4 %convolution_convert_fusion = bf16[2048,2048]{1,0:T(8,128)(2,1)} fusion(bf16[896,2048]{1,0:T(8,128)(2,1)} %param.23, f32[896,2048]{1,0:T(8,128)} %fusion.154, s32[2048]{0:T(1024)S(1)} %copy-done.58, s32[896]{0:T(1024)S(1)} %copy-done.63), kind=kOutput, calls=%fused_computation.31 | convolution fusion | flops 7529562112 | bytes 19410432 | tf_op jit(solution)/shard_map/dot_general | solution.py:235
  776.1 15.1 %convolution_convert_fusion.1 = bf16[2048,2048]{1,0:T(8,128)(2,1)} fusion(bf16[896,2048]{1,0:T(8,128)(2,1)} %fusion.29, f32[896,2048]{1,0:T(8,128)} %copy-done.3, f32[2048]{0:T(1024)S(1)} %copy-done.45, f32[896]{0:T(1024)S(1)} %add_rsqrt_fusion, f32[896]{0:T(1024)S(1)} %broadcast_multiply_fusion.6), kind=kOutput, calls=%fused_computation.32 | convolution fusion | flops 7527727104 | bytes 19414016 | tf_op jit(solution)/shard_map/dot_general | solution.py:236
  799.9 14.7 all_gather.51
  833.7 15.8 %all_gather.55 = f32[2,4,2048]{2,1,0:T(4,128)} all-gather(f32[2,4,256]{2,1,0:T(4,128)S(1)} %bitcast.162), channel_id=1, replica_groups=mesh['heads'=4,'seq'=8] {'seq'}, dimensions={2}, use_global_device_ids=true | all-gather | bytes 73728 | tf_op jit(solution)/shard_map/all_gather | solution.py:273
  872.7 13.8 multiply_reduce_fusion
  886.5 14.8 fusion.74
  901.6 15.1 %all_gather.53 = f32[3,4,1024]{2,1,0:T(4,128)S(1)} all-gather(f32[3,4,128]{2,1,0:T(4,128)S(1)} %get-tuple-element.61), channel_id=1, replica_groups=mesh['heads'=4,'seq'=8] {'seq'}, dimensions={2}, use_global_device_ids=true | all-gather | bytes 55296 | tf_op jit(solution)/shard_map/all_gather | solution.py:274
  916.7 15.4 %all_gather.57 = f32[2,4,2048]{2,1,0:T(4,128)} all-gather(f32[2,4,256]{2,1,0:T(4,128)S(1)} %get-tuple-element.59), channel_id=1, replica_groups=mesh['heads'=4,'seq'=8] {'seq'}, dimensions={2}, use_global_device_ids=true | all-gather | bytes 73728 | tf_op jit(solution)/shard_map/all_gather | solution.py:274
  966.0 13.0 fusion.72
  1010.4 15.1 %convolution_convert_fusion.3 = bf16[896,2048]{1,0:T(8,128)(2,1)} fusion(bf16[2048,2048]{1,0:T(8,128)(2,1)} %all-gather.21.cloned.1.call-done, f32[896,2048]{1,0:T(8,128)} %fusion.154, s32[2048]{0:T(1024)S(1)} %copy-done.59, s32[896]{0:T(1024)S(1)} %copy-done.64), kind=kOutput, calls=%fused_computation.73 | convolution fusion | flops 7527202816 | bytes 19410432 | tf_op jit(solution)/shard_map/dot_general | solution.py:219
  1041.9 28.2 %psum.67 = bf16[5,2048]{1,0:T(8,128)(2,1)S(1)} all-reduce(bf16[5,2048]{1,0:T(8,128)(2,1)S(1)} %fusion.55), channel_id=1, replica_groups=mesh['heads'=4,'seq'=8] {'seq'}, use_global_device_ids=true, to_apply=%region_18.19 | all-reduce | flops 10240 | bytes 40960 | tf_op jit(solution)/shard_map/psum | solution.py:189
  1074.9 22.1 %reduce-scatter.3.cloned.1.call-done = bf16[256,2048]{1,0:T(8,128)(2,1)} async-done(((bf16[2048,2048]{1,0:T(8,128)(2,1)}), bf16[256,2048]{1,0:T(8,128)(2,1)}) %reduce-scatter.3.cloned.1.call-update) | async-done | bytes 1048592 | tf_op jit(solution)/shard_map/reduce_scatter | solution.py:241
  1099.8 173.5 %all-reduce.12.cloned.1.call-done = (bf16[2048,3,512]{2,0,1:T(8,128)(2,1)}, bf16[512,2048]{1,0:T(8,128)(2,1)}) async-done(((bf16[2048,3,512]{2,0,1:T(8,128)(2,1)}, bf16[512,2048]{1,0:T(8,128)(2,1)}), (bf16[2048,3,512]{2,0,1:T(8,128)(2,1)}, bf16[512,2048]{1,0:T(8,128)(2,1)})) %all-reduce.12.cloned.1.call-update) | async-done | bytes 8388624 | tf_op jit(solution)/shard_map/psum | solution.py:322
  1284.8 148.0 %all-reduce.14.cloned.1.call-done = (bf16[896,2048]{1,0:T(8,128)(2,1)}, bf16[896,2048]{1,0:T(8,128)(2,1)}) async-done(((bf16[896,2048]{1,0:T(8,128)(2,1)}, bf16[896,2048]{1,0:T(8,128)(2,1)}), (bf16[896,2048]{1,0:T(8,128)(2,1)}, bf16[896,2048]{1,0:T(8,128)(2,1)})) %all-reduce.14.cloned.1.call-update) | async-done | bytes 7340048 | tf_op jit(solution)/shard_map/psum | solution.py:220
  1449.5 16.5 %all-reduce = (bf16[2048]{0:T(1024)(128)(2,1)S(1)}, bf16[2048]{0:T(1024)(128)(2,1)S(1)}) all-reduce(bf16[2048]{0:T(1024)(128)(2,1)S(1)} %get-tuple-element.11, bf16[2048]{0:T(1024)(128)(2,1)S(1)} %copy-done.52), channel_id=1, replica_groups=mesh['heads'=4,'seq'=8] {'seq'}, use_global_device_ids=true, to_apply=%region_30.31 | all-reduce | flops 4096 | bytes 16384 | tf_op jit(solution)/shard_map/psum | solution.py:324
  (311 shorter events, 371.6 us)
Async XLA Ops:
  7.2 225.8 %copy-start = (bf16[512,2048]{1,0:T(8,128)(2,1)S(1)}, bf16[512,2048]{1,0:T(8,128)(2,1)}, u32[]{:S(2)}) copy-start(bf16[512,2048]{1,0:T(8,128)(2,1)} %param.14) | copy-start | bytes 6291460
  7.2 69.3 %all-gather.11.cloned.1.call-start = ((), (), s32[]{:S(2)}) async-start(), calls=%async_computation.2 | async-start | bytes 3538944 | tf_op jit(solution)/shard_map/all_gather | solution.py:51
  35.4 80.4 %all-gather.13.cloned.1.call-start = ((), (), s32[]{:S(2)}) async-start(), calls=%async_computation.3 | async-start | bytes 3538944 | tf_op jit(solution)/shard_map/all_gather | solution.py:50
  57.9 105.9 %all-gather.17.cloned.1.call-start = ((), (), s32[]{:S(2)}) async-start(), calls=%async_computation.5 | async-start | bytes 4718592 | tf_op jit(solution)/shard_map/all_gather | solution.py:50
  61.7 149.3 %all-gather.15.cloned.1.call-start = ((), (), s32[]{:S(2)}) async-start(), calls=%async_computation.4 | async-start | bytes 4718592 | tf_op jit(solution)/shard_map/all_gather | solution.py:51
  63.6 330.0 %all-reduce.8.cloned.1.call-start = ((), (), s32[]{:S(2)}) async-start(), calls=%async_computation.6 | async-start | bytes 14680064 | tf_op jit(solution)/shard_map/psum | solution.py:210
  63.9 168.0 %copy-start.69 = (s32[512]{0:T(512)}, s32[512]{0:T(512)S(1)}, u32[]{:S(2)}) copy-start(s32[512]{0:T(512)S(1)} %fusion.125) | copy-start | bytes 6148
  68.7 163.3 %copy-start.65 = (s32[896]{0:T(1024)}, s32[896]{0:T(1024)S(1)}, u32[]{:S(2)}) copy-start(s32[896]{0:T(1024)S(1)} %broadcast_multiply_fusion.1) | copy-start | bytes 10756
  68.8 57.0 %copy-start.11 = (pred[128,1024]{1,0:T(8,128)(4,1)}, pred[128,1024]{1,0:T(8,128)(4,1)S(1)}, u32[]{:S(2)}) copy-start(pred[128,1024]{1,0:T(8,128)(4,1)S(1)} %iota_compare_fusion.3) | copy-start | bytes 393220
  239.3 237.9 %all-gather.19.cloned.1.call-start = ((), (), s32[]{:S(2)}) async-start(), calls=%async_computation.7 | async-start | bytes 9437184 | tf_op jit(solution)/shard_map/all_gather | solution.py:214
  239.8 319.9 %all-gather.21.cloned.1.call-start = ((), (), s32[]{:S(2)}) async-start(), calls=%async_computation.8 | async-start | bytes 9437184 | tf_op jit(solution)/shard_map/all_gather | solution.py:215
  240.6 499.3 %all-reduce.10.cloned.1.call-start = ((), (), s32[]{:S(2)}) async-start(), calls=%async_computation.9 | async-start | bytes 14680064 | tf_op jit(solution)/shard_map/psum | solution.py:237
  240.7 319.1 %copy-start.57 = (s32[2048]{0:T(1024)}, s32[2048]{0:T(1024)S(1)}, u32[]{:S(2)}) copy-start(s32[2048]{0:T(1024)S(1)} %iota_add_fusion) | copy-start | bytes 24580
  240.7 319.1 %copy-start.62 = (s32[896]{0:T(1024)}, s32[896]{0:T(1024)S(1)}, u32[]{:S(2)}) copy-start(s32[896]{0:T(1024)S(1)} %broadcast_multiply_fusion) | copy-start | bytes 10756
  398.6 78.6 %copy-start.44 = (f32[2048]{0:T(1024)S(1)}, f32[2048]{0:T(1024)}, u32[]{:S(2)}) copy-start(f32[2048]{0:T(1024)} %param.18) | copy-start | bytes 24580
  586.1 209.2 %all-gather.23.cloned.1.call-start = ((), (), s32[]{:S(2)}) async-start(), calls=%async_computation.10 | async-start | bytes 3538944 | tf_op jit(solution)/shard_map/all_gather | solution.py:269
  590.0 237.3 %all-gather.27.cloned.1.call-start = ((), (), s32[]{:S(2)}) async-start(), calls=%async_computation.12 | async-start | bytes 4718592 | tf_op jit(solution)/shard_map/all_gather | solution.py:269
  593.3 154.0 %copy-start.45 = (f32[2048]{0:T(1024)S(1)}, f32[2048]{0:T(1024)}, u32[]{:S(2)}) copy-start(f32[2048]{0:T(1024)} %param.18) | copy-start | bytes 24580
  593.3 346.1 %all-gather.25.cloned.1.call-start = ((), (), s32[]{:S(2)}) async-start(), calls=%async_computation.11 | async-start | bytes 3538944 | tf_op jit(solution)/shard_map/all_gather | solution.py:270
  758.4 197.6 %all-gather.29.cloned.1.call-start = ((), (), s32[]{:S(2)}) async-start(), calls=%async_computation.13 | async-start | bytes 4718592 | tf_op jit(solution)/shard_map/all_gather | solution.py:270
  760.6 311.6 %reduce-scatter.5.cloned.1.call-start = ((), (), s32[]{:S(2)}) async-start(), calls=%async_computation.15 | async-start | bytes 9437184 | tf_op jit(solution)/shard_map/reduce_scatter | solution.py:244
  776.1 320.9 %reduce-scatter.3.cloned.1.call-start = ((), (), s32[]{:S(2)}) async-start(), calls=%async_computation.14 | async-start | bytes 9437184 | tf_op jit(solution)/shard_map/reduce_scatter | solution.py:241
  791.3 482.0 %all-reduce.12.cloned.1.call-start = ((), (), s32[]{:S(2)}) async-start(), calls=%async_computation.16 | async-start | bytes 16777216 | tf_op jit(solution)/shard_map/psum | solution.py:322
  1009.7 423.1 %all-reduce.14.cloned.1.call-start = ((), (), s32[]{:S(2)}) async-start(), calls=%async_computation.17 | async-start | bytes 14680064 | tf_op jit(solution)/shard_map/psum | solution.py:220
  (66 other events, 647.8 us)
Sparse Core Ops, SparseCore 0:
  35.5 40.9 all-gather.10
  78.6 37.1 all-gather.12
  118.0 45.7 all-gather.16
  165.2 45.6 all-gather.14
  239.4 154.2 all-reduce.7
  395.1 82.0 all-gather.18
  478.7 80.9 all-gather.20
  586.2 153.6 all-reduce.9
  741.5 38.1 all-gather.22
  781.2 46.1 all-gather.26
  829.0 40.0 all-gather.24
  871.1 44.4 all-gather.28
  917.9 87.9 reduce-scatter.4
  1008.6 88.2 reduce-scatter.2
  1099.2 174.0 all-reduce.11
  1277.2 155.5 all-reduce.13
where the time goes:
time: 1490 us; the launch traced here: 1480 us
  waiting for transfers between devices  891 us (60%)
  matrix products  268 us (18%)
  local copies, waits for them, and re-layouts  115 us (8%)
  blocking collectives  106 us (7%)
  other arithmetic  88.5 us (6%)
  between operations  15.1 us (1%)
    psum x1, waiting for transfers between devices, local(): lax.psum(grad_qkv_part.astype(jnp.bfloat16), 'seq').astype(jnp.float32)  174 us
    psum x1, waiting for transfers between devices, local(): hidden = tokens_wide + lax.psum(attn_part, 'heads')  153 us
    psum x1, waiting for transfers between devices, local(): lax.psum(ffn_part.astype(jnp.bfloat16), 'heads').astype(jnp.float32)  148 us
    psum x1, waiting for transfers between devices, local(): lax.psum(jnp.dot(grad_upward, back_up.T, preferred_element_type=jnp.float...  146 us
    all_gather x1, waiting for transfers between devices, local(): lax.all_gather(w_up, 'seq', axis=0, tiled=True)  74.7 us
    all_gather x1, waiting for transfers between devices, local(): lax.all_gather(w_down, 'seq', axis=1, tiled=True)  67.9 us
    all_gather x2, waiting for transfers between devices, gather_rows(): lax.all_gather(keys, 'seq', axis=1, tiled=True)  64.2 us
    unnamed x153, local copies, waits for them, and re-layouts  34.3 us
  transfers between devices with their start and end apart: 16, of which 12 were waited for; matrix products, arithmetic and copies ran while one was open for 23% of the time, Pallas kernels for 0%

commit v1 on v0

--- a/solution.py
+++ b/solution.py
@@ -14,6 +14,19 @@
 SEQS = 5
 epsilon = 1e-05
 highest = lax.Precision.HIGHEST
+
+
+def ring_gather(shard, axis, dim):
+    ways = lax.axis_size(axis)
+    up = [(d, (d + 1) % ways) for d in range(ways)]
+    down = [(d, (d - 1) % ways) for d in range(ways)]
+    earlier, later = ([shard], [shard])
+    for _ in range(ways // 2):
+        earlier.append(lax.ppermute(earlier[-1], axis, up))
+    for _ in range((ways - 1) // 2):
+        later.append(lax.ppermute(later[-1], axis, down))
+    line = jnp.concatenate([*earlier[::-1], *later[1:]], axis=dim)
+    return jnp.roll(line, (lax.axis_index(axis) - ways // 2) * shard.shape[dim], axis=dim)
 
 
 def normalize_parts(values):
@@ -211,7 +224,7 @@
     hat_two, inverse_two = normalize_parts(hidden)
     normed_two = (hat_two * gain_ffn).astype(jnp.bfloat16)
     full_up, full_down = (
-        lax.all_gather(w_up, "seq", axis=0, tiled=True),
+        ring_gather(w_up, "seq", 0),
         lax.all_gather(w_down, "seq", axis=1, tiled=True),
     )
     upward = jnp.dot(normed_two, full_up, preferred_element_type=jnp.float32)

time: 1490 us -> 1560 us (1.047)
  local copies, waits for them, and re-layouts: 115 us -> 142 us
  waiting for transfers between devices: 891 us -> 910 us
    ppermute x0 -> x7, waiting for transfers between devices: none -> 122 us  [the longest x4 118 us: ring_gather(): earlier.append(lax.ppermute(earlier[-1], axis, up))]
    psum x1, waiting for transfers between devices: 174 us -> 97.7 us  [local(): lax.psum(grad_qkv_part.astype(jnp.bfloat16), 'seq').astype(jnp.float32)]
    unnamed x153 -> x178, local copies, waits for them, and re-layouts: 34.3 us -> 63.8 us
    reduce_scatter x1, waiting for transfers between devices: 22.1 us -> 0.01 us  [local(): lax.psum_scatter(grad_up_part.astype(jnp.bfloat16), 'seq', scatter_dimens...]
  transfers between devices with their start and end apart: 16 -> 23, of which waited for: 12 -> 15; matrix products, arithmetic and copies ran while one was open for 23% -> 24% of each run, Pallas kernels for 0% -> 0%
where the time goes in v1:
time: 1560 us; the launch traced here: 1550 us
  waiting for transfers between devices  910 us (58%)
  matrix products  273 us (18%)
  local copies, waits for them, and re-layouts  142 us (9%)
  blocking collectives  107 us (7%)
  other arithmetic  93 us (6%)
    psum x1, waiting for transfers between devices, local(): hidden = tokens_wide + lax.psum(attn_part, 'heads')  153 us
    psum x1, waiting for transfers between devices, local(): lax.psum(jnp.dot(grad_upward, back_up.T, preferred_element_type=jnp.float...  150 us
    psum x1, waiting for transfers between devices, local(): lax.psum(ffn_part.astype(jnp.bfloat16), 'heads').astype(jnp.float32)  148 us
    ppermute x4, waiting for transfers between devices, ring_gather(): earlier.append(lax.ppermute(earlier[-1], axis, up))  118 us
    psum x1, waiting for transfers between devices, local(): lax.psum(grad_qkv_part.astype(jnp.bfloat16), 'seq').astype(jnp.float32)  97.7 us
    all_gather x1, waiting for transfers between devices, local(): lax.all_gather(w_up, 'seq', axis=0, tiled=True)  72.7 us
    all_gather x1, waiting for transfers between devices, local(): lax.all_gather(w_down, 'seq', axis=1, tiled=True)  69.5 us
    all_gather x2, waiting for transfers between devices, gather_rows(): lax.all_gather(keys, 'seq', axis=1, tiled=True)  64.2 us
  transfers between devices with their start and end apart: 23, of which 15 were waited for; matrix products, arithmetic and copies ran while one was open for 24% of the time, Pallas kernels for 0%

profile of v1, /device:TPU:0, one launch (start us, length us, event | category | flops | bytes accessed | tf_op | source)
XLA Modules:
  0.0 1551.7 jit_solution(1811007774868459381)
XLA Ops:
  81.2 34.6 %all-gather.13.cloned.1.call-done = bf16[3,1024,512]{2,1,0:T(8,128)(2,1)} async-done(((bf16[3,128,512]{2,1,0:T(8,128)(2,1)}), bf16[3,1024,512]{2,1,0:T(8,128)(2,1)}) %all-gather.13.cloned.1.call-update) | async-done | bytes 3145744 | tf_op jit(solution)/shard_map/all_gather | solution.py:63
  134.2 29.5 %all-gather.17.cloned.1.call-done = bf16[2,2048,512]{2,1,0:T(8,128)(2,1)} async-done(((bf16[2,256,512]{2,1,0:T(8,128)(2,1)}), bf16[2,2048,512]{2,1,0:T(8,128)(2,1)}) %all-gather.17.cloned.1.call-update) | async-done | bytes 4194320 | tf_op jit(solution)/shard_map/all_gather | solution.py:63
  185.7 25.3 %all-gather.15.cloned.1.call-done = bf16[2,2048,512]{2,1,0:T(8,128)(2,1)} async-done(((bf16[2,256,512]{2,1,0:T(8,128)(2,1)}), bf16[2,2048,512]{2,1,0:T(8,128)(2,1)}) %all-gather.15.cloned.1.call-update) | async-done | bytes 4194320 | tf_op jit(solution)/shard_map/all_gather | solution.py:64
  240.8 152.9 %all-reduce.8.cloned.1.call-done = f32[896,2048]{1,0:T(8,128)} async-done(((f32[896,2048]{1,0:T(8,128)}), f32[896,2048]{1,0:T(8,128)}) %all-reduce.8.cloned.1.call-update) | async-done | bytes 7340048 | tf_op jit(solution)/shard_map/psum | solution.py:223
  404.6 72.7 %all-gather.21.cloned.1.call-done = bf16[2048,2048]{1,0:T(8,128)(2,1)} async-done(((bf16[256,2048]{1,0:T(8,128)(2,1)}), bf16[2048,2048]{1,0:T(8,128)(2,1)}) %all-gather.21.cloned.1.call-update) | async-done | bytes 8388624 | tf_op jit(solution)/shard_map/all_gather | solution.py:237
  490.3 69.5 %all-gather.19.cloned.1.call-done = bf16[2048,2048]{1,0:T(8,128)(2,1)} async-done(((bf16[2048,256]{1,0:T(8,128)(2,1)}), bf16[2048,2048]{1,0:T(8,128)(2,1)}) %all-gather.19.cloned.1.call-update) | async-done | bytes 8388624 | tf_op jit(solution)/shard_map/all_gather | solution.py:228
  559.8 15.0 fusion.31
  590.0 150.0 %all-reduce.10.cloned.1.call-done = f32[896,2048]{1,0:T(8,128)} async-done(((f32[896,2048]{1,0:T(8,128)}), f32[896,2048]{1,0:T(8,128)}) %all-reduce.10.cloned.1.call-update) | async-done | bytes 7340048 | tf_op jit(solution)/shard_map/psum | solution.py:250
  758.7 15.3 convolution_convert_fusion
  775.3 16.1 %collective-permute-done = bf16[256,2048]{1,0:T(8,128)(2,1)S(1)} collective-permute-done((bf16[256,2048]{1,0:T(8,128)(2,1)S(1)}, bf16[256,2048]{1,0:T(8,128)(2,1)S(1)}, u32[]{:S(2)}, u32[]{:S(2)}) %collective-permute-start) | collective-permute-done | bytes 1048608 | tf_op jit(solution)/shard_map/ppermute | solution.py:25
  794.9 46.1 %collective-permute-done.1 = bf16[256,2048]{1,0:T(8,128)(2,1)S(1)} collective-permute-done((bf16[256,2048]{1,0:T(8,128)(2,1)S(1)}, bf16[256,2048]{1,0:T(8,128)(2,1)S(1)}, u32[]{:S(2)}, u32[]{:S(2)}) %collective-permute-start.1) | collective-permute-done | bytes 1048608 | tf_op jit(solution)/shard_map/ppermute | solution.py:25
  844.6 24.3 %collective-permute-done.2 = bf16[256,2048]{1,0:T(8,128)(2,1)} collective-permute-done((bf16[256,2048]{1,0:T(8,128)(2,1)S(1)}, bf16[256,2048]{1,0:T(8,128)(2,1)}, u32[]{:S(2)}, u32[]{:S(2)}) %collective-permute-start.2) | collective-permute-done | bytes 1048608 | tf_op jit(solution)/shard_map/ppermute | solution.py:25
  880.4 31.5 %collective-permute-done.3 = bf16[256,2048]{1,0:T(8,128)(2,1)} collective-permute-done((bf16[256,2048]{1,0:T(8,128)(2,1)}, bf16[256,2048]{1,0:T(8,128)(2,1)}, u32[]{:S(2)}, u32[]{:S(2)}) %collective-permute-start.3) | collective-permute-done | bytes 1048608 | tf_op jit(solution)/shard_map/ppermute | solution.py:25
  960.0 19.8 %all_gather.50 = f32[3,4,1024]{2,1,0:T(4,128)S(1)} all-gather(f32[3,4,128]{2,1,0:T(4,128)S(1)} %log_add_fusion.1), channel_id=1, replica_groups=mesh['heads'=4,'seq'=8] {'seq'}, dimensions={2}, use_global_device_ids=true | all-gather | bytes 55296 | tf_op jit(solution)/shard_map/all_gather | solution.py:286
  992.0 14.4 all_gather.54
  1029.6 13.4 multiply_reduce_fusion
  1043.0 14.8 fusion.91
  1071.3 14.4 all_gather.56
  1120.6 13.6 fusion.89
  1165.6 24.3 %fusion.54 = bf16[896,2048]{1,0:T(8,128)(2,1)} fusion(bf16[2048,2048]{1,0:T(8,128)(2,1)} %all-gather.19.cloned.1.call-done, bf16[896,2048]{1,0:T(8,128)(2,1)} %multiply_convert_fusion.4, bf16[4096,2048]{1,0:T(8,128)(2,1)} %constant_dynamic-update-slice_fusion, s32[]{:T(128)S(6)} %select_n.135, s32[2048]{0:T(1024)S(1)} %copy-done.61, s32[896]{0:T(1024)S(1)} %copy-done.65), kind=kOutput, calls=%fused_computation.83 | convolution fusion | flops 15043395584 | bytes 24129028 | tf_op jit(solution)/shard_map/dot_general | solution.py:232
  1206.3 29.1 %psum.67 = bf16[5,2048]{1,0:T(8,128)(2,1)S(1)} all-reduce(bf16[5,2048]{1,0:T(8,128)(2,1)S(1)} %fusion.72), channel_id=1, replica_groups=mesh['heads'=4,'seq'=8] {'seq'}, use_global_device_ids=true, to_apply=%region_18.19 | all-reduce | flops 10240 | bytes 40960 | tf_op jit(solution)/shard_map/psum | solution.py:202
  1242.9 97.7 %all-reduce.12.cloned.1.call-done = (bf16[2048,3,512]{2,0,1:T(8,128)(2,1)}, bf16[512,2048]{1,0:T(8,128)(2,1)}) async-done(((bf16[2048,3,512]{2,0,1:T(8,128)(2,1)}, bf16[512,2048]{1,0:T(8,128)(2,1)}), (bf16[2048,3,512]{2,0,1:T(8,128)(2,1)}, bf16[512,2048]{1,0:T(8,128)(2,1)})) %all-reduce.12.cloned.1.call-update) | async-done | bytes 8388624 | tf_op jit(solution)/shard_map/psum | solution.py:335
  1352.1 148.0 %all-reduce.14.cloned.1.call-done = (bf16[896,2048]{1,0:T(8,128)(2,1)}, bf16[896,2048]{1,0:T(8,128)(2,1)}) async-done(((bf16[896,2048]{1,0:T(8,128)(2,1)}, bf16[896,2048]{1,0:T(8,128)(2,1)}), (bf16[896,2048]{1,0:T(8,128)(2,1)}, bf16[896,2048]{1,0:T(8,128)(2,1)})) %all-reduce.14.cloned.1.call-update) | async-done | bytes 7340048 | tf_op jit(solution)/shard_map/psum | solution.py:233
  1516.9 16.5 %all-reduce = (bf16[2048]{0:T(1024)(128)(2,1)S(1)}, bf16[2048]{0:T(1024)(128)(2,1)S(1)}) all-reduce(bf16[2048]{0:T(1024)(128)(2,1)S(1)} %get-tuple-element.11, bf16[2048]{0:T(1024)(128)(2,1)S(1)} %copy-done.53), channel_id=1, replica_groups=mesh['heads'=4,'seq'=8] {'seq'}, use_global_device_ids=true, to_apply=%region_30.31 | all-reduce | flops 4096 | bytes 16384 | tf_op jit(solution)/shard_map/psum | solution.py:337
  (352 shorter events, 447.5 us)
Async XLA Ops:
  7.2 69.3 %all-gather.11.cloned.1.call-start = ((), (), s32[]{:S(2)}) async-start(), calls=%async_computation.2 | async-start | bytes 3538944 | tf_op jit(solution)/shard_map/all_gather | solution.py:64
  35.4 80.4 %all-gather.13.cloned.1.call-start = ((), (), s32[]{:S(2)}) async-start(), calls=%async_computation.3 | async-start | bytes 3538944 | tf_op jit(solution)/shard_map/all_gather | solution.py:63
  57.9 105.9 %all-gather.17.cloned.1.call-start = ((), (), s32[]{:S(2)}) async-start(), calls=%async_computation.5 | async-start | bytes 4718592 | tf_op jit(solution)/shard_map/all_gather | solution.py:63
  61.6 149.3 %all-gather.15.cloned.1.call-start = ((), (), s32[]{:S(2)}) async-start(), calls=%async_computation.4 | async-start | bytes 4718592 | tf_op jit(solution)/shard_map/all_gather | solution.py:64
  63.6 330.1 %all-reduce.8.cloned.1.call-start = ((), (), s32[]{:S(2)}) async-start(), calls=%async_computation.6 | async-start | bytes 14680064 | tf_op jit(solution)/shard_map/psum | solution.py:223
  239.4 237.9 %all-gather.21.cloned.1.call-start = ((), (), s32[]{:S(2)}) async-start(), calls=%async_computation.8 | async-start | bytes 9437184 | tf_op jit(solution)/shard_map/all_gather | solution.py:237
  239.9 319.9 %all-gather.19.cloned.1.call-start = ((), (), s32[]{:S(2)}) async-start(), calls=%async_computation.7 | async-start | bytes 9437184 | tf_op jit(solution)/shard_map/all_gather | solution.py:228
  240.7 499.3 %all-reduce.10.cloned.1.call-start = ((), (), s32[]{:S(2)}) async-start(), calls=%async_computation.9 | async-start | bytes 14680064 | tf_op jit(solution)/shard_map/psum | solution.py:250
  240.8 319.1 %copy-start.59 = (s32[2048]{0:T(1024)}, s32[2048]{0:T(1024)S(1)}, u32[]{:S(2)}) copy-start(s32[2048]{0:T(1024)S(1)} %iota_add_fusion) | copy-start | bytes 24580
  586.2 369.1 %all-gather.23.cloned.1.call-start = ((), (), s32[]{:S(2)}) async-start(), calls=%async_computation.10 | async-start | bytes 3538944 | tf_op jit(solution)/shard_map/all_gather | solution.py:282
  588.4 397.1 %all-gather.27.cloned.1.call-start = ((), (), s32[]{:S(2)}) async-start(), calls=%async_computation.12 | async-start | bytes 4718592 | tf_op jit(solution)/shard_map/all_gather | solution.py:282
  589.9 503.4 %all-gather.25.cloned.1.call-start = ((), (), s32[]{:S(2)}) async-start(), calls=%async_computation.11 | async-start | bytes 3538944 | tf_op jit(solution)/shard_map/all_gather | solution.py:283
  757.5 352.4 %all-gather.29.cloned.1.call-start = ((), (), s32[]{:S(2)}) async-start(), calls=%async_computation.13 | async-start | bytes 4718592 | tf_op jit(solution)/shard_map/all_gather | solution.py:283
  758.6 478.8 %reduce-scatter.5.cloned.1.call-start = ((), (), s32[]{:S(2)}) async-start(), calls=%async_computation.15 | async-start | bytes 9437184 | tf_op jit(solution)/shard_map/reduce_scatter | solution.py:257
  774.1 466.0 %reduce-scatter.3.cloned.1.call-start = ((), (), s32[]{:S(2)}) async-start(), calls=%async_computation.14 | async-start | bytes 9437184 | tf_op jit(solution)/shard_map/reduce_scatter | solution.py:254
  775.3 16.1 %collective-permute-start = (bf16[256,2048]{1,0:T(8,128)(2,1)S(1)}, bf16[256,2048]{1,0:T(8,128)(2,1)S(1)}, u32[]{:S(2)}, u32[]{:S(2)}) collective-permute-start(bf16[256,2048]{1,0:T(8,128)(2,1)S(1)} %copy-done.15), channel_id=1, source_target_pairs={{0,1},{1,2},{2,3},{3,4},{4,5},{5,6},{6,7},{7,0},{8,9},{9,10},{10,1... | collective-permute-start | bytes 3145736 | tf_op jit(solution)/shard_map/ppermute | solution.py:25
  791.4 49.7 %collective-permute-start.1 = (bf16[256,2048]{1,0:T(8,128)(2,1)S(1)}, bf16[256,2048]{1,0:T(8,128)(2,1)S(1)}, u32[]{:S(2)}, u32[]{:S(2)}) collective-permute-start(bf16[256,2048]{1,0:T(8,128)(2,1)S(1)} %collective-permute-done), channel_id=1, source_target_pairs={{0,1},{1,2},{2,3},{3,4},{4,5},{5,6},{6,7},{7,0},{8,9},{9,10},{10,1... | collective-permute-start | bytes 3145736 | tf_op jit(solution)/shard_map/ppermute | solution.py:25
  791.4 49.7 %collective-permute-start.4 = (bf16[256,2048]{1,0:T(8,128)(2,1)S(1)}, bf16[256,2048]{1,0:T(8,128)(2,1)}, u32[]{:S(2)}, u32[]{:S(2)}) collective-permute-start(bf16[256,2048]{1,0:T(8,128)(2,1)S(1)} %copy-done.15), channel_id=1, source_target_pairs={{0,7},{1,0},{2,1},{3,2},{4,3},{5,4},{6,5},{7,6},{8,15},{9,8},{10,9... | collective-permute-start | bytes 3145736 | tf_op jit(solution)/shard_map/ppermute | solution.py:27
  841.1 27.8 %collective-permute-start.2 = (bf16[256,2048]{1,0:T(8,128)(2,1)S(1)}, bf16[256,2048]{1,0:T(8,128)(2,1)}, u32[]{:S(2)}, u32[]{:S(2)}) collective-permute-start(bf16[256,2048]{1,0:T(8,128)(2,1)S(1)} %collective-permute-done.1), channel_id=1, source_target_pairs={{0,1},{1,2},{2,3},{3,4},{4,5},{5,6},{6,7},{7,0},{8,9},{9,10},{10,1... | collective-permute-start | bytes 3145736 | tf_op jit(solution)/shard_map/ppermute | solution.py:25
  842.0 34.7 %collective-permute-start.5 = (bf16[256,2048]{1,0:T(8,128)(2,1)}, bf16[256,2048]{1,0:T(8,128)(2,1)}, u32[]{:S(2)}, u32[]{:S(2)}) collective-permute-start(bf16[256,2048]{1,0:T(8,128)(2,1)} %collective-permute-done.4), channel_id=1, source_target_pairs={{0,7},{1,0},{2,1},{3,2},{4,3},{5,4},{6,5},{7,6},{8,15},{9,8},{10,9... | collective-permute-start | bytes 3145736 | tf_op jit(solution)/shard_map/ppermute | solution.py:27
  868.9 43.1 %collective-permute-start.3 = (bf16[256,2048]{1,0:T(8,128)(2,1)}, bf16[256,2048]{1,0:T(8,128)(2,1)}, u32[]{:S(2)}, u32[]{:S(2)}) collective-permute-start(bf16[256,2048]{1,0:T(8,128)(2,1)} %collective-permute-done.2), channel_id=1, source_target_pairs={{0,1},{1,2},{2,3},{3,4},{4,5},{5,6},{6,7},{7,0},{8,9},{9,10},{10,1... | collective-permute-start | bytes 3145736 | tf_op jit(solution)/shard_map/ppermute | solution.py:25
  876.7 61.2 %collective-permute-start.6 = (bf16[256,2048]{1,0:T(8,128)(2,1)}, bf16[256,2048]{1,0:T(8,128)(2,1)}, u32[]{:S(2)}, u32[]{:S(2)}) collective-permute-start(bf16[256,2048]{1,0:T(8,128)(2,1)} %collective-permute-done.5), channel_id=1, source_target_pairs={{0,7},{1,0},{2,1},{3,2},{4,3},{5,4},{6,5},{7,6},{8,15},{9,8},{10,9... | collective-permute-start | bytes 3145736 | tf_op jit(solution)/shard_map/ppermute | solution.py:27
  937.8 402.8 %all-reduce.12.cloned.1.call-start = ((), (), s32[]{:S(2)}) async-start(), calls=%async_computation.16 | async-start | bytes 16777216 | tf_op jit(solution)/shard_map/psum | solution.py:335
  1165.0 335.2 %all-reduce.14.cloned.1.call-start = ((), (), s32[]{:S(2)}) async-start(), calls=%async_computation.17 | async-start | bytes 14680064 | tf_op jit(solution)/shard_map/psum | solution.py:233
  (78 other events, 1719.5 us)
Sparse Core Ops, SparseCore 0:
  35.5 40.9 all-gather.10
  78.7 37.1 all-gather.12
  118.0 45.7 all-gather.16
  165.2 45.6 all-gather.14
  239.5 154.2 all-reduce.7
  395.2 82.0 all-gather.20
  478.8 80.9 all-gather.18
  586.3 153.6 all-reduce.9
  741.6 38.1 all-gather.22
  781.3 67.3 all-gather.26
  850.3 61.2 all-gather.24
  913.1 47.7 all-gather.28
  963.1 88.6 reduce-scatter.4
  1054.5 88.9 reduce-scatter.2
  1165.1 175.4 all-reduce.11
  1344.6 155.5 all-reduce.13
